TPU v7x, 256 devices: a whole 4x4x8 slice. The times are simulated.
256 devices in a mesh: blk: 8 (over x, core), uly: 8 (over z), tp: 4 (over y).
Axes of the slice: x: 4, y: 4, z: 8, core: 2. Of those that a mesh axis runs over, the one named last changes fastest.
Arguments:
- hidden: bfloat16 [8192, 8192], P(('blk', 'uly')), may hold values from -8 to 8
- norm_gain: bfloat16 [8192], replicated, may hold values from 0.099609375 to 1.8984375
- query_key_value_weight: bfloat16 [8192, 4, 1280], P('uly', 'tp'), may hold values from -1 to 1
- w_out: bfloat16 [4096, 8192], P('tp', 'uly'), may hold values from -0.5 to 0.5
- doc_ids: int32 [8192], replicated, may hold values from 0 to 15, never falling along the last dimension, each value on 1 to 2048 neighbouring positions
- block_order: int32 [16], replicated, may hold values from 0 to 15, each once
Outputs:
- attn_out: bfloat16 [8192, 8192], P(('blk', 'tp'), 'uly')
Inputs may be any that keep to these rules, and one draw needn't show every extreme that they name: `doc_ids`: never falls along the sequence; every document holds 1 to 2048 positions and one holds exactly 2048. Array rows c * 512 to (c + 1) * 512 - 1 hold sequence block block_order[c]; every block appears once.
All inputs are finite; a program needn't handle non-finite values.
Results may differ from a plain program's by a relative error of at most 0.029.
Values may be sent and summed in bfloat16 or wider, within the bound.
A program may use at most 64 MiB of HBM per device.

v0:
```python
import math
import jax
import jax.numpy as jnp
from jax import lax
from jax.sharding import PartitionSpec as P

QUERY_HEAD_COUNT = 32
KV_HEAD_COUNT = 4
HEAD_SIZE = 128
BLOCK = 512
THETA = 500000.0
NEG_BIG = -1e30


def rope_tables(positions):
    half_dim = HEAD_SIZE // 2
    lane_ids = jnp.arange(half_dim).astype(jnp.float32)
    base_freq = jnp.power(THETA, -2.0 * lane_ids / HEAD_SIZE)
    wavelen = 2.0 * math.pi / base_freq
    smooth = (8192.0 / wavelen - 1.0) / 3.0
    blended = (1.0 - smooth) * base_freq / 8.0 + smooth * base_freq
    scaled = jnp.where(
        wavelen > 8192.0, base_freq / 8.0, jnp.where(wavelen < 2048.0, base_freq, blended)
    )
    angles = positions.astype(jnp.float32)[:, None] * scaled[None, :]
    return (jnp.cos(angles), jnp.sin(angles))


def rotate(values, cos_table, sin_table):
    half_dim = values.shape[-1] // 2
    leading = values[..., :half_dim]
    trailing = values[..., half_dim:]
    cos_part = cos_table[:, None, :]
    sin_part = sin_table[:, None, :]
    return jnp.concatenate(
        [leading * cos_part - trailing * sin_part, trailing * cos_part + leading * sin_part],
        axis=-1,
    )


def positions_of(block_order, row_ids):
    block_ids = row_ids // BLOCK
    matches = block_ids[:, None] == jnp.arange(block_order.shape[0])[None, :]
    seq_block = jnp.sum(jnp.where(matches, block_order[None, :], 0), axis=1)
    return seq_block * BLOCK + row_ids % BLOCK


def make_attend(queries, query_pos, query_seg, doc_ids, block_order):
    head_dim = queries.shape[2]
    inv_root = 1.0 / math.sqrt(head_dim)

    def attend(running, pieces, offset):
        key_piece, value_piece = pieces
        key_count = key_piece.shape[0]
        block_size = key_count
        while block_size > 1024 and block_size % 2 == 0:
            block_size = block_size // 2
        block_total = key_count // block_size
        piece_pos = positions_of(block_order, jnp.arange(key_count))
        piece_seg = jnp.take(doc_ids, piece_pos)
        stacked = (
            key_piece.reshape(block_total, block_size, head_dim),
            value_piece.reshape(block_total, block_size, head_dim),
            piece_pos.reshape(block_total, block_size),
            piece_seg.reshape(block_total, block_size),
        )

        def one_block(softmax_state, block_data):
            key_blk, value_blk, pos_blk, seg_blk = block_data
            allowed = (pos_blk[None, :] <= query_pos[:, None]) & (
                seg_blk[None, :] == query_seg[:, None]
            )
            row_max, row_sum, weighted = softmax_state
            scores = (
                jnp.einsum("qhd,kd->hqk", queries, key_blk, preferred_element_type=jnp.float32)
                * inv_root
            )
            scores = jnp.where(allowed[None, :, :], scores, NEG_BIG)
            new_max = jnp.maximum(row_max, jnp.max(scores, axis=2))
            weights = jnp.where(allowed[None, :, :], jnp.exp(scores - new_max[:, :, None]), 0.0)
            factor = jnp.exp(row_max - new_max)
            new_sum = row_sum * factor + jnp.sum(weights, axis=2)
            product = jnp.einsum(
                "hqk,kd->hqd",
                weights.astype(jnp.bfloat16),
                value_blk,
                preferred_element_type=jnp.float32,
            )
            next_state = (new_max, new_sum, weighted * factor[:, :, None] + product)
            return (next_state, None)

        final_state, unused = lax.scan(one_block, running, stacked)
        return final_state

    return attend


def on_device(hidden, norm_gain, query_key_value_weight, w_out, doc_ids, block_order):
    group_width = QUERY_HEAD_COUNT // KV_HEAD_COUNT
    heads_here = group_width // lax.axis_size("uly")
    widened = hidden.astype(jnp.float32)
    inverse_rms = lax.rsqrt(jnp.mean(widened * widened, axis=1, keepdims=True) + 1e-05)
    rms_scaled = (widened * inverse_rms * norm_gain.astype(jnp.float32)[None, :]).astype(
        jnp.bfloat16
    )
    regrouped = lax.all_to_all(rms_scaled, "uly", split_axis=1, concat_axis=0, tiled=True)
    block_len = regrouped.shape[0]
    local_weights = query_key_value_weight.reshape(
        query_key_value_weight.shape[0], (group_width + 2) * HEAD_SIZE
    )
    partial_proj = jnp.dot(regrouped, local_weights, preferred_element_type=jnp.float32)
    query_part = partial_proj[:, : group_width * HEAD_SIZE]
    pair_part = partial_proj[:, group_width * HEAD_SIZE :]
    first_row = lax.axis_index("blk") * block_len
    query_pos = positions_of(block_order, first_row + jnp.arange(block_len))
    query_seg = jnp.take(doc_ids, query_pos)
    cos_query, sin_query = rope_tables(query_pos)
    query_sum, pair_sum = (
        lax.psum_scatter(query_part, "uly", scatter_dimension=1, tiled=True),
        lax.psum_scatter(pair_part, "uly", scatter_dimension=0, tiled=True),
    )
    key_len = pair_sum.shape[0]
    key_start = first_row + lax.axis_index("uly") * key_len
    key_pos = positions_of(block_order, key_start + jnp.arange(key_len))
    cos_key, sin_key = rope_tables(key_pos)
    queries = rotate(
        query_sum.reshape(block_len, heads_here, HEAD_SIZE), cos_query, sin_query
    ).astype(jnp.bfloat16)
    keys_local = rotate(pair_sum[:, None, :HEAD_SIZE], cos_key, sin_key)[:, 0, :].astype(
        jnp.bfloat16
    )
    values_local = pair_sum[:, HEAD_SIZE:].astype(jnp.bfloat16)
    attend = make_attend(queries, query_pos, query_seg, doc_ids, block_order)
    initial = (
        jnp.full((heads_here, block_len), NEG_BIG, jnp.float32),
        jnp.zeros((heads_here, block_len), jnp.float32),
        jnp.zeros((heads_here, block_len, HEAD_SIZE), jnp.float32),
    )
    final_state = attend(
        initial,
        (
            lax.all_gather(keys_local, ("blk", "uly"), axis=0, tiled=True),
            lax.all_gather(values_local, ("blk", "uly"), axis=0, tiled=True),
        ),
        jnp.int32(0),
    )
    row_max, row_sum, weighted = final_state
    attended = (weighted / row_sum[:, :, None]).astype(jnp.bfloat16)
    head_weights = w_out.reshape(group_width, HEAD_SIZE, w_out.shape[1])
    projected_rows = jnp.einsum(
        "hqd,hdn->qn",
        lax.all_gather(attended, "uly", axis=0, tiled=True),
        head_weights,
        preferred_element_type=jnp.float32,
    )
    return lax.psum_scatter(
        projected_rows.astype(jnp.bfloat16), "tp", scatter_dimension=0, tiled=True
    )


def solution(mesh):
    return jax.shard_map(
        on_device,
        mesh=mesh,
        in_specs=(P(("blk", "uly"), None), P(), P("uly", "tp", None), P("tp", "uly"), P(), P()),
        out_specs=P(("blk", "tp"), "uly"),
        check_vma=False,
    )
```

profile of v0, /device:TPU:1, one launch (start us, length us, event | category | flops | bytes accessed | tf_op | source)
XLA Modules:
  0.0 473.3 jit_solution(8503466636216364546)
XLA Ops:
  7.4 4.1 copy.14
  14.2 4.6 fusion.28
  18.8 58.6 %all_to_all.19 = bf16[128,8,1024]{0,2,1:T(8,128)(2,1)} all-to-all(bf16[128,8,1024]{0,2,1:T(8,128)(2,1)S(1)} %bitcast.99), channel_id=1, replica_groups=mesh['blk'=8,'uly'=8,'tp'=4] {'uly'}, dimensions={1} | all-to-all | bytes 4194304 | tf_op jit(solution)/shard_map/all_to_all | solution.py:106
  77.4 3.9 copy.15
  81.3 4.7 fusion.29
  89.6 32.3 %reduce-scatter.4.cloned.1.call-done = f32[128,256]{0,1:T(8,128)} async-done(((f32[1024,256]{0,1:T(8,128)}), f32[128,256]{0,1:T(8,128)}) %reduce-scatter.4.cloned.1.call-update) | async-done | bytes 131088 | tf_op jit(solution)/shard_map/reduce_scatter | solution.py:120
  125.1 4.8 %slice.41 = f32[1024,1024]{0,1:T(8,128)} slice(f32[1024,1280]{0,1:T(8,128)} %copy-done.2), slice={[0:1024], [0:1024]} | slice | bytes 8388608 | tf_op jit(solution)/shard_map/slice | solution.py:112
  130.7 6.1 %gather_fusion.1 = s32[1024]{0:T(1024)S(1)} fusion(s32[8192]{0:T(1024)S(1)} %copy-done.1, s32[1024]{0:T(1024)S(1)} %broadcast_clamp_fusion.1), kind=kCustom, calls=%fused_computation.1 | custom fusion | bytes 12288 | tf_op jit(solution)/shard_map/jit(_take)/gather | solution.py:116
  136.9 45.5 %gather_fusion = s32[8192]{0:T(1024)S(1)} fusion(s32[8192]{0:T(1024)S(1)} %copy-done.1, s32[8192]{0:T(1024)S(1)} %broadcast_clamp_fusion), kind=kCustom, calls=%fused_computation | custom fusion | bytes 98304 | tf_op jit(solution)/shard_map/jit(_take)/gather | solution.py:60
  182.5 17.9 %all-gather.9.cloned.1.call-done = bf16[8192,1,128]{0,2,1:T(8,128)(2,1)} async-done(((bf16[128,1,128]{0,2,1:T(8,128)(2,1)}), bf16[8192,1,128]{0,2,1:T(8,128)(2,1)}) %all-gather.9.cloned.1.call-update) | async-done | bytes 2097168 | tf_op jit(solution)/shard_map/all_gather | solution.py:142
  200.4 4.1 copy.22
  204.5 69.9 %all-gather.5.cloned.1.call-done = bf16[8192,128]{0,1:T(8,128)(2,1)} async-done(((bf16[128,128]{0,1:T(8,128)(2,1)}), bf16[8192,128]{0,1:T(8,128)(2,1)}) %all-gather.5.cloned.1.call-update) | async-done | bytes 2097168 | tf_op jit(solution)/shard_map/all_gather | solution.py:143
  274.4 4.1 copy.23
  278.5 52.2 %reduce-scatter.6.cloned.1.call-done = f32[1024,128]{0,1:T(8,128)} async-done(((f32[1024,1024]{0,1:T(8,128)}), f32[1024,128]{0,1:T(8,128)}) %reduce-scatter.6.cloned.1.call-update) | async-done | bytes 524304 | tf_op jit(solution)/shard_map/reduce_scatter | solution.py:119
  333.7 55.2 %while.15 = (s32[]{:T(128)}, f32[1,1024]{1,0:T(1,128)S(1)}, f32[1,1024]{1,0:T(1,128)S(1)}, f32[1,1024,128]{2,1,0:T(8,128)S(1)}, s32[8,1024]{1,0:T(8,128)S(1)}, /...) while((s32[]{:T(128)}, f32[1,1024]{1,0:T(1,128)S(1)}, ...), condition=%wide.region_9.10_spmd.clone, body=%wide.region_6.9_spmd.clone.sunk | while | flops 560337920 | bytes 14549149 | solution.py:92
  344.6 2.8 fusion.81
  351.5 2.8 fusion.81
  358.4 2.8 fusion.81
  365.3 2.8 fusion.81
  372.2 2.8 fusion.81
  386.1 2.8 fusion.81
  389.9 36.0 %all-gather.7.cloned.1.call-done = bf16[8,1024,128]{2,1,0:T(8,128)(2,1)} async-done(((bf16[1,1024,128]{2,1,0:T(8,128)(2,1)}), bf16[8,1024,128]{2,1,0:T(8,128)(2,1)}) %all-gather.7.cloned.1.call-update) | async-done | bytes 2097168 | tf_op jit(solution)/shard_map/all_gather | solution.py:152
  425.9 5.9 %bitcast_convert_fusion = bf16[1024,1024]{1,0:T(8,128)(2,1)} fusion(bf16[8,1024,128]{2,1,0:T(8,128)(2,1)} %all-gather.7.cloned.1.call-done, bf16[8,128,1024]{2,1,0:T(8,128)(2,1)} %bitcast.121), kind=kOutput, calls=%fused_computation.37 | convolution fusion | flops 2148532224 | bytes 6291456 | tf_op jit(solution)/shard_map/hqd,hdn->qn/dot_general | solution.py:150
  431.8 34.7 %reduce-scatter.8.cloned.1.call-done = bf16[256,1024]{1,0:T(8,128)(2,1)} async-done(((bf16[1024,1024]{1,0:T(8,128)(2,1)}), bf16[256,1024]{1,0:T(8,128)(2,1)}) %reduce-scatter.8.cloned.1.call-update) | async-done | bytes 524304 | tf_op jit(solution)/shard_map/reduce_scatter | solution.py:156
  (103 shorter events, 53.0 us)
Async XLA Ops:
  6.5 74.7 %copy-start = (bf16[1024,1,1280]{2,0,1:T(8,128)(2,1)S(1)}, bf16[1024,1,1280]{2,0,1:T(8,128)(2,1)}, u32[]{:S(2)}) copy-start(bf16[1024,1,1280]{2,0,1:T(8,128)(2,1)} %param.10) | copy-start | bytes 7864324
  6.5 115.3 %reduce-scatter.4.cloned.1.call-start = ((), (), s32[]{:S(2)}) async-start(), calls=%async_computation.4 | async-start | bytes 1179648 | tf_op jit(solution)/shard_map/reduce_scatter | solution.py:120
  81.3 8.2 %copy-start.3 = (s32[16]{0:T(128)S(1)}, s32[16]{0:T(128)}, u32[]{:S(2)}) copy-start(s32[16]{0:T(128)} %param.13) | copy-start | bytes 196
  86.0 2.3 copy-start.2
  89.3 111.1 %all-gather.9.cloned.1.call-start = ((), (), s32[]{:S(2)}) async-start(), calls=%async_computation.9 | async-start | bytes 2129920 | tf_op jit(solution)/shard_map/all_gather | solution.py:142
  123.5 150.9 %all-gather.5.cloned.1.call-start = ((), (), s32[]{:S(2)}) async-start(), calls=%async_computation.6 | async-start | bytes 2129920 | tf_op jit(solution)/shard_map/all_gather | solution.py:143
  125.1 205.6 %reduce-scatter.6.cloned.1.call-start = ((), (), s32[]{:S(2)}) async-start(), calls=%async_computation.5 | async-start | bytes 4718592 | tf_op jit(solution)/shard_map/reduce_scatter | solution.py:119
  129.9 0.8 copy-start.1
  129.9 296.0 %all-gather.7.cloned.1.call-start = ((), (), s32[]{:S(2)}) async-start(), calls=%async_computation.7 | async-start | bytes 2359296 | tf_op jit(solution)/shard_map/all_gather | solution.py:152
  389.8 76.7 %reduce-scatter.8.cloned.1.call-start = ((), (), s32[]{:S(2)}) async-start(), calls=%async_computation.8 | async-start | bytes 2621440 | tf_op jit(solution)/shard_map/reduce_scatter | solution.py:156
Sparse Core Ops, SparseCore 0:
  89.5 32.3 reduce-scatter.3
  124.4 75.9 all-gather.8
  203.0 71.3 all-gather.4
  276.8 53.8 reduce-scatter.5
  389.9 35.9 all-gather.6
  431.9 34.5 reduce-scatter.7
where the time goes:
time: 474 us; the launch traced here: 473 us
  waiting for transfers between devices  243 us (51%)
  local copies, waits for them, and re-layouts  79.3 us (17%)
  blocking collectives  58.6 us (12%)
  matrix products  51.9 us (11%)
  other arithmetic  25.8 us (5%)
  between operations  13.7 us (3%)
    all_gather x1, waiting for transfers between devices, on_device(): lax.all_gather(values_local, ('blk', 'uly'), axis=0, tiled=True)  69.9 us
    all_to_all x1, blocking collectives, on_device(): lax.all_to_all(rms_scaled, 'uly', split_axis=1, concat_axis=0, tiled=True)  58.6 us
    reduce_scatter x1, waiting for transfers between devices, on_device(): lax.psum_scatter(query_part, 'uly', scatter_dimension=1, tiled=True)  52.2 us
    gather x2, local copies, waits for them, and re-layouts, attend(): piece_seg = jnp.take(doc_ids, piece_pos)  45.5 us
    all_gather x1, waiting for transfers between devices, on_device(): lax.all_gather(attended, 'uly', axis=0, tiled=True)  36 us
    reduce_scatter x1, waiting for transfers between devices, on_device(): lax.psum_scatter(projected_rows.astype(jnp.bfloat16), 'tp', scatter_dimen...  34.7 us
    reduce_scatter x1, waiting for transfers between devices, on_device(): lax.psum_scatter(pair_part, 'uly', scatter_dimension=0, tiled=True)  32.3 us
    dot_general x8, matrix products, one_block(): jnp.einsum('hqk,kd->hqd', weights.astype(jnp.bfloat16), value_blk, prefer...  22.4 us
  transfers between devices with their start and end apart: 6, of which 6 were waited for; matrix products, arithmetic and copies ran while one was open for 14% of the time, Pallas kernels for 0%

commit v1 on v0

--- a/solution.py
+++ b/solution.py
@@ -10,6 +10,22 @@
 BLOCK = 512
 THETA = 500000.0
 NEG_BIG = -1e30
+
+
+def ring_product(value, axis, dim, term):
+    peers, place, rows = (lax.axis_size(axis), lax.axis_index(axis), value.shape[dim])
+    forward = [(i, (i + 1) % peers) for i in range(peers)]
+    left = [(i, (i - 1) % peers) for i in range(peers)]
+    middle = peers // 2
+    from_left = from_right = value
+    total = term(value, place * rows)
+    for step in range(1, middle + 1):
+        from_left = lax.ppermute(from_left, axis, forward)
+        if step < peers - middle:
+            from_right = lax.ppermute(from_right, axis, left)
+            total = total + term(from_right, (place + step) % peers * rows)
+        total = total + term(from_left, (place - step) % peers * rows)
+    return total
 
 
 def rope_tables(positions):
@@ -147,11 +163,16 @@
     row_max, row_sum, weighted = final_state
     attended = (weighted / row_sum[:, :, None]).astype(jnp.bfloat16)
     head_weights = w_out.reshape(group_width, HEAD_SIZE, w_out.shape[1])
-    projected_rows = jnp.einsum(
-        "hqd,hdn->qn",
-        lax.all_gather(attended, "uly", axis=0, tiled=True),
-        head_weights,
-        preferred_element_type=jnp.float32,
+    projected_rows = ring_product(
+        attended,
+        "uly",
+        0,
+        lambda own_block, start: jnp.einsum(
+            "hqd,hdn->qn",
+            own_block,
+            lax.dynamic_slice_in_dim(head_weights, start, own_block.shape[0], axis=0),
+            preferred_element_type=jnp.float32,
+        ),
     )
     return lax.psum_scatter(
         projected_rows.astype(jnp.bfloat16), "tp", scatter_dimension=0, tiled=True

time: 474 us -> 468 us (0.987)
  waiting for transfers between devices: 243 us -> 218 us
  matrix products: 51.9 us -> 64.3 us
  starting transfers between devices: 0.39 us -> 8.45 us
    all_gather x1 -> x0, waiting for transfers between devices: 36 us -> none  [on_device(): lax.all_gather(attended, 'uly', axis=0, tiled=True)]
    dot_general x1 -> x8, matrix products: 5.86 us -> 19.1 us  [on_device(): jnp.einsum('hqd,hdn->qn', own_block, lax.dynamic_slice_in_dim(head_weight...]
    ppermute x0 -> x7, waiting for transfers between devices: none -> 10 us  [the longest x4 10 us: ring_product(): from_left = lax.ppermute(from_left, axis, forward)]
    ppermute x0 -> x7, starting transfers between devices: none -> 8.1 us  [the longest x3 8.01 us: ring_product(): from_right = lax.ppermute(from_right, axis, left)]
    unnamed x12 -> x16, local copies, waits for them, and re-layouts: 15.4 us -> 14.7 us
  transfers between devices with their start and end apart: 6 -> 12, of which waited for: 6 -> 9; matrix products, arithmetic and copies ran while one was open for 14% -> 17% of each run, Pallas kernels for 0% -> 0%
where the time goes in v1:
time: 468 us; the launch traced here: 467 us
  waiting for transfers between devices  218 us (47%)
  local copies, waits for them, and re-layouts  78.6 us (17%)
  matrix products  64.3 us (14%)
  blocking collectives  58.6 us (13%)
  other arithmetic  25.1 us (5%)
  between operations  13.6 us (3%)
  starting transfers between devices  8.45 us (2%)
    all_gather x1, waiting for transfers between devices, on_device(): lax.all_gather(values_local, ('blk', 'uly'), axis=0, tiled=True)  69.9 us
    all_to_all x1, blocking collectives, on_device(): lax.all_to_all(rms_scaled, 'uly', split_axis=1, concat_axis=0, tiled=True)  58.6 us
    reduce_scatter x1, waiting for transfers between devices, on_device(): lax.psum_scatter(query_part, 'uly', scatter_dimension=1, tiled=True)  52.2 us
    gather x2, local copies, waits for them, and re-layouts, attend(): piece_seg = jnp.take(doc_ids, piece_pos)  45.5 us
    reduce_scatter x1, waiting for transfers between devices, on_device(): lax.psum_scatter(projected_rows.astype(jnp.bfloat16), 'tp', scatter_dimen...  35.2 us
    reduce_scatter x1, waiting for transfers between devices, on_device(): lax.psum_scatter(pair_part, 'uly', scatter_dimension=0, tiled=True)  32.3 us
    dot_general x8, matrix products, one_block(): jnp.einsum('hqk,kd->hqd', weights.astype(jnp.bfloat16), value_blk, prefer...  22.4 us
    dot_general x8, matrix products, on_device(): jnp.einsum('hqd,hdn->qn', own_block, lax.dynamic_slice_in_dim(head_weight...  19.1 us
  transfers between devices with their start and end apart: 12, of which 9 were waited for; matrix products, arithmetic and copies ran while one was open for 17% of the time, Pallas kernels for 0%

profile of v1, /device:TPU:1, one launch (start us, length us, event | category | flops | bytes accessed | tf_op | source)
XLA Modules:
  0.0 466.7 jit_solution(15015871772600722391)
XLA Ops:
  7.4 4.1 copy.12
  14.2 4.6 fusion.28
  18.8 58.6 %all_to_all.19 = bf16[128,8,1024]{0,2,1:T(8,128)(2,1)} all-to-all(bf16[128,8,1024]{0,2,1:T(8,128)(2,1)S(1)} %bitcast.143), channel_id=1, replica_groups=mesh['blk'=8,'uly'=8,'tp'=4] {'uly'}, dimensions={1} | all-to-all | bytes 4194304 | tf_op jit(solution)/shard_map/all_to_all | solution.py:122
  77.4 3.9 copy.13
  81.3 4.7 %fusion.29 = f32[1024,1280]{0,1:T(8,128)S(1)} fusion(bf16[1024,1024]{1,0:T(8,128)(2,1)} %bitcast.155, bf16[1024,1,1280]{2,0,1:T(8,128)(2,1)S(1)} %copy-done), kind=kOutput, calls=%fused_computation.38 | convolution fusion | flops 2684354560 | bytes 9961472 | tf_op jit(solution)/shard_map/dot_general | solution.py:127
  89.6 32.3 %reduce-scatter.4.cloned.1.call-done = f32[128,256]{0,1:T(8,128)} async-done(((f32[1024,256]{0,1:T(8,128)}), f32[128,256]{0,1:T(8,128)}) %reduce-scatter.4.cloned.1.call-update) | async-done | bytes 131088 | tf_op jit(solution)/shard_map/reduce_scatter | solution.py:136
  125.1 4.8 %slice.41 = f32[1024,1024]{0,1:T(8,128)} slice(f32[1024,1280]{0,1:T(8,128)} %copy-done.3), slice={[0:1024], [0:1024]} | slice | bytes 8388608 | tf_op jit(solution)/shard_map/slice | solution.py:128
  130.7 6.2 %gather_fusion.1 = s32[1024]{0:T(1024)S(1)} fusion(s32[8192]{0:T(1024)S(1)} %copy-done.2, s32[1024]{0:T(1024)S(1)} %broadcast_clamp_fusion.1), kind=kCustom, calls=%fused_computation.1 | custom fusion | bytes 12288 | tf_op jit(solution)/shard_map/jit(_take)/gather | solution.py:132
  137.0 45.5 %gather_fusion = s32[8192]{0:T(1024)S(1)} fusion(s32[8192]{0:T(1024)S(1)} %copy-done.2, s32[8192]{0:T(1024)S(1)} %broadcast_clamp_fusion), kind=kCustom, calls=%fused_computation | custom fusion | bytes 98304 | tf_op jit(solution)/shard_map/jit(_take)/gather | solution.py:76
  182.6 17.9 %all-gather.6.cloned.1.call-done = bf16[8192,1,128]{0,2,1:T(8,128)(2,1)} async-done(((bf16[128,1,128]{0,2,1:T(8,128)(2,1)}), bf16[8192,1,128]{0,2,1:T(8,128)(2,1)}) %all-gather.6.cloned.1.call-update) | async-done | bytes 2097168 | tf_op jit(solution)/shard_map/all_gather | solution.py:158
  200.5 4.1 copy.20
  204.6 69.9 %all-gather.4.cloned.1.call-done = bf16[8192,128]{0,1:T(8,128)(2,1)} async-done(((bf16[128,128]{0,1:T(8,128)(2,1)}), bf16[8192,128]{0,1:T(8,128)(2,1)}) %all-gather.4.cloned.1.call-update) | async-done | bytes 2097168 | tf_op jit(solution)/shard_map/all_gather | solution.py:159
  274.5 4.1 copy.21
  278.5 52.2 %reduce-scatter.6.cloned.1.call-done = f32[1024,128]{0,1:T(8,128)} async-done(((f32[1024,1024]{0,1:T(8,128)}), f32[1024,128]{0,1:T(8,128)}) %reduce-scatter.6.cloned.1.call-update) | async-done | bytes 524304 | tf_op jit(solution)/shard_map/reduce_scatter | solution.py:135
  333.1 54.4 %while.15 = (s32[]{:T(128)}, f32[1,1024]{1,0:T(1,128)S(1)}, f32[1,1024]{1,0:T(1,128)S(1)}, f32[1,1024,128]{2,1,0:T(8,128)S(1)}, s32[8,1024]{1,0:T(8,128)S(1)}, /...) while((s32[]{:T(128)}, f32[1,1024]{1,0:T(1,128)S(1)}, ...), condition=%wide.region_9.10_spmd.clone, body=%wide.region_6.9_spmd.clone.sunk | while | flops 560337920 | bytes 14549149 | solution.py:108
  337.2 2.8 fusion.118
  344.0 2.8 fusion.118
  350.8 2.8 fusion.118
  364.3 2.8 fusion.118
  377.9 2.8 fusion.118
  391.2 5.1 %collective-permute-done.1 = bf16[1,1024,128]{2,1,0:T(8,128)(2,1)S(1)} collective-permute-done((bf16[1,1024,128]{2,1,0:T(8,128)(2,1)S(1)}, bf16[1,1024,128]{2,1,0:T(8,128)(2,1)S(1)}, u32[]{:S(2)}, u32[]{:S(2)}) %collective-permute-start.1) | collective-permute-done | bytes 262176 | tf_op jit(solution)/shard_map/ppermute | solution.py:23
  400.3 3.4 collective-permute-done.3
  416.6 8.3 %add_convert_fusion = bf16[1024,1024]{1,0:T(8,128)(2,1)} fusion(f32[1024,1024]{1,0:T(8,128)} %fusion.41, f32[1024,1024]{1,0:T(8,128)} %fusion.44, f32[1024,1024]{1,0:T(8,128)} %fusion.47, f32[1024,1024]{1,0:T(8,128)S(1)} %fusion.50, f32[1024,1024]{1,0:T(8,128)S(1)} %fusion.53, f32[1024,1024]{1,0:T(8,128)S(1)} %fusion.59, f32[1024,1024]{1,0:T(8,128)S(1)} %fusion.56, ...), kind=kOutput, calls=%fused_computation.37 | convolution fusion | flops 276824064 | bytes 31981572 | tf_op jit(solution)/shard_map/hqd,hdn->qn/dot_general | solution.py:170
  425.0 35.2 %reduce-scatter.8.cloned.1.call-done = bf16[256,1024]{1,0:T(8,128)(2,1)} async-done(((bf16[1024,1024]{1,0:T(8,128)(2,1)}), bf16[256,1024]{1,0:T(8,128)(2,1)}) %reduce-scatter.8.cloned.1.call-update) | async-done | bytes 524304 | tf_op jit(solution)/shard_map/reduce_scatter | solution.py:177
  (125 shorter events, 73.9 us)
Async XLA Ops:
  6.5 74.7 %copy-start = (bf16[1024,1,1280]{2,0,1:T(8,128)(2,1)S(1)}, bf16[1024,1,1280]{2,0,1:T(8,128)(2,1)}, u32[]{:S(2)}) copy-start(bf16[1024,1,1280]{2,0,1:T(8,128)(2,1)} %param.10) | copy-start | bytes 7864324
  6.5 115.3 %reduce-scatter.4.cloned.1.call-start = ((), (), s32[]{:S(2)}) async-start(), calls=%async_computation.4 | async-start | bytes 1179648 | tf_op jit(solution)/shard_map/reduce_scatter | solution.py:136
  81.3 8.2 %copy-start.5 = (s32[16]{0:T(128)S(1)}, s32[16]{0:T(128)}, u32[]{:S(2)}) copy-start(s32[16]{0:T(128)} %param.13) | copy-start | bytes 196
  86.0 2.3 copy-start.3
  89.3 111.2 %all-gather.6.cloned.1.call-start = ((), (), s32[]{:S(2)}) async-start(), calls=%async_computation.8 | async-start | bytes 2129920 | tf_op jit(solution)/shard_map/all_gather | solution.py:158
  123.5 150.9 %all-gather.4.cloned.1.call-start = ((), (), s32[]{:S(2)}) async-start(), calls=%async_computation.6 | async-start | bytes 2129920 | tf_op jit(solution)/shard_map/all_gather | solution.py:159
  125.1 205.7 %reduce-scatter.6.cloned.1.call-start = ((), (), s32[]{:S(2)}) async-start(), calls=%async_computation.5 | async-start | bytes 4718592 | tf_op jit(solution)/shard_map/reduce_scatter | solution.py:135
  129.9 0.8 copy-start.2
  129.9 330.2 %reduce-scatter.8.cloned.1.call-start = ((), (), s32[]{:S(2)}) async-start(), calls=%async_computation.7 | async-start | bytes 2621440 | tf_op jit(solution)/shard_map/reduce_scatter | solution.py:177
  333.1 57.4 %copy-start.4 = (bf16[1024,1024]{1,0:T(8,128)(2,1)S(1)}, bf16[1024,1024]{1,0:T(8,128)(2,1)}, u32[]{:S(2)}) copy-start(bf16[1024,1024]{1,0:T(8,128)(2,1)} %param.11) | copy-start | bytes 6291460
  387.7 8.5 %collective-permute-start.1 = (bf16[1,1024,128]{2,1,0:T(8,128)(2,1)S(1)}, bf16[1,1024,128]{2,1,0:T(8,128)(2,1)S(1)}, u32[]{:S(2)}, u32[]{:S(2)}) collective-permute-start(bf16[1,1024,128]{2,1,0:T(8,128)(2,1)S(1)} %divide_convert_fusion), channel_id=1, source_target_pairs={{0,4},{4,8},{8,12},{12,16},{16,20},{20,24},{24,28},{28,0},{1,5},{5... | collective-permute-start | bytes 786440 | tf_op jit(solution)/shard_map/ppermute | solution.py:23
  387.8 8.4 %collective-permute-start = (bf16[1,1024,128]{2,1,0:T(8,128)(2,1)S(1)}, bf16[1,1024,128]{2,1,0:T(8,128)(2,1)S(1)}, u32[]{:S(2)}, u32[]{:S(2)}) collective-permute-start(bf16[1,1024,128]{2,1,0:T(8,128)(2,1)S(1)} %divide_convert_fusion), channel_id=1, source_target_pairs={{0,28},{4,0},{8,4},{12,8},{16,12},{20,16},{24,20},{28,24},{1,29},{... | collective-permute-start | bytes 786440 | tf_op jit(solution)/shard_map/ppermute | solution.py:25
  396.2 7.5 %collective-permute-start.3 = (bf16[1,1024,128]{2,1,0:T(8,128)(2,1)S(1)}, bf16[1,1024,128]{2,1,0:T(8,128)(2,1)S(1)}, u32[]{:S(2)}, u32[]{:S(2)}) collective-permute-start(bf16[1,1024,128]{2,1,0:T(8,128)(2,1)S(1)} %collective-permute-done.1), channel_id=1, source_target_pairs={{0,4},{4,8},{8,12},{12,16},{16,20},{20,24},{24,28},{28,0},{1,5},{5... | collective-permute-start | bytes 786440 | tf_op jit(solution)/shard_map/ppermute | solution.py:23
  396.2 7.5 %collective-permute-start.2 = (bf16[1,1024,128]{2,1,0:T(8,128)(2,1)S(1)}, bf16[1,1024,128]{2,1,0:T(8,128)(2,1)S(1)}, u32[]{:S(2)}, u32[]{:S(2)}) collective-permute-start(bf16[1,1024,128]{2,1,0:T(8,128)(2,1)S(1)} %collective-permute-done), channel_id=1, source_target_pairs={{0,28},{4,0},{8,4},{12,8},{16,12},{20,16},{24,20},{28,24},{1,29},{... | collective-permute-start | bytes 786440 | tf_op jit(solution)/shard_map/ppermute | solution.py:25
  403.8 6.4 %collective-permute-start.5 = (bf16[1,1024,128]{2,1,0:T(8,128)(2,1)S(1)}, bf16[1,1024,128]{2,1,0:T(8,128)(2,1)S(1)}, u32[]{:S(2)}, u32[]{:S(2)}) collective-permute-start(bf16[1,1024,128]{2,1,0:T(8,128)(2,1)S(1)} %collective-permute-done.3), channel_id=1, source_target_pairs={{0,4},{4,8},{8,12},{12,16},{16,20},{20,24},{24,28},{28,0},{1,5},{5... | collective-permute-start | bytes 786440 | tf_op jit(solution)/shard_map/ppermute | solution.py:23
  403.8 9.1 %collective-permute-start.4 = (bf16[1,1024,128]{2,1,0:T(8,128)(2,1)S(1)}, bf16[1,1024,128]{2,1,0:T(8,128)(2,1)S(1)}, u32[]{:S(2)}, u32[]{:S(2)}) collective-permute-start(bf16[1,1024,128]{2,1,0:T(8,128)(2,1)S(1)} %collective-permute-done.2), channel_id=1, source_target_pairs={{0,28},{4,0},{8,4},{12,8},{16,12},{20,16},{24,20},{28,24},{1,29},{... | collective-permute-start | bytes 786440 | tf_op jit(solution)/shard_map/ppermute | solution.py:25
  410.2 6.4 %collective-permute-start.6 = (bf16[1,1024,128]{2,1,0:T(8,128)(2,1)S(1)}, bf16[1,1024,128]{2,1,0:T(8,128)(2,1)S(1)}, u32[]{:S(2)}, u32[]{:S(2)}) collective-permute-start(bf16[1,1024,128]{2,1,0:T(8,128)(2,1)S(1)} %collective-permute-done.5), channel_id=1, source_target_pairs={{0,4},{4,8},{8,12},{12,16},{16,20},{20,24},{24,28},{28,0},{1,5},{5... | collective-permute-start | bytes 786440 | tf_op jit(solution)/shard_map/ppermute | solution.py:23
  416.6 43.5 %copy-start.1 = (bf16[1024,1,1280]{2,0,1:T(8,128)(2,1)S(1)}, bf16[1024,1,1280]{2,0,1:T(8,128)(2,1)}, u32[]{:S(2)}) copy-start(bf16[1024,1,1280]{2,0,1:T(8,128)(2,1)} %param.10) | copy-start | bytes 7864324
Sparse Core Ops, SparseCore 0:
  89.5 32.3 reduce-scatter.3
  124.4 76.0 all-gather.5
  203.1 71.3 all-gather.3
  276.9 53.8 reduce-scatter.5
  425.1 34.9 reduce-scatter.7
